TPU v7x, 32 devices: a whole 2x2x4 slice. The times are simulated.
32 devices in a mesh: vel: 16 (over z, y, x), space: 2 (over core).
Axes of the slice: x: 2, y: 2, z: 4, core: 2. Of those that a mesh axis runs over, the one named last changes fastest.
Arguments:
- distribution: float32 [16384, 16, 128], P('vel', 'space'), may hold values from 0 to 11, as said below
- rate_class: int32 [16, 128], P('space'), may hold values from 0 to 7
- boundary_obstacle_indicator: int32 [16, 128], P('space'), may hold values 0 or 1
Outputs:
- field_out: float32 [16384, 16, 128], P('vel', 'space')
- latest_conserved_fields: float32 [5, 16, 128], P(None, 'space')
Inputs may be any that keep to these rules, and one draw needn't show every extreme that they name: `distribution`: every entry positive.
All inputs are finite; a program needn't handle non-finite values. No bound on the sum of `boundary_obstacle_indicator` on one device may be relied on, other than what follows from the above.
Results may differ from a plain program's by a relative error of at most 0.0003.
Values sent between devices are 32-bit elements; how exact they have to be, the bound alone decides.
A program may use at most 64 MiB of HBM per device.

v0:
```python
import jax
import jax.numpy as jnp
from jax import lax
from jax.sharding import PartitionSpec as P

VX = 32
VY = 32
VZ = 16
ITERS = 2
SWEEPS = 4
speed_edge = 5.0
marching_step_length = 0.1
momentum_thermal_ratio = 2.0 / 3.0
shear_power_law_index = 0.81
diffusivity = 1.0


def with_halo(value, sides, width):
    for axis, dim in sides:
        size, length = (lax.axis_size(axis), value.shape[dim])
        up = [(i, (i + 1) % size) for i in range(size)]
        down = [(j, i) for i, j in up]
        last = lax.slice_in_dim(value, length - width, length, axis=dim)
        leading = lax.slice_in_dim(value, 0, width, axis=dim)
        before = lax.ppermute(last, axis, up)
        after = lax.ppermute(leading, axis, down)
        value = jnp.concatenate([before, value, after], axis=dim)
    return value


def velocity_table(index):
    index_x = index % VX
    index_y = index // VX % VY
    index_z = index // (VX * VY)
    discrete_abscissa_xaxis = -speed_edge + (index_x.astype(jnp.float32) + 0.5) * (
        2.0 * speed_edge / VX
    )
    discrete_abscissa_yaxis = -speed_edge + (index_y.astype(jnp.float32) + 0.5) * (
        2.0 * speed_edge / VY
    )
    discrete_abscissa_zaxis = -speed_edge + (index_z.astype(jnp.float32) + 0.5) * (
        2.0 * speed_edge / VZ
    )
    return (discrete_abscissa_xaxis, discrete_abscissa_yaxis, discrete_abscissa_zaxis)


def moment_weights(discrete_abscissa_xaxis, discrete_abscissa_yaxis, discrete_abscissa_zaxis):
    square = (
        discrete_abscissa_xaxis * discrete_abscissa_xaxis
        + discrete_abscissa_yaxis * discrete_abscissa_yaxis
        + discrete_abscissa_zaxis * discrete_abscissa_zaxis
    )
    quadrature = (
        2.0
        * speed_edge
        / VX
        * (2.0 * speed_edge / VY)
        * (2.0 * speed_edge / VZ)
        / (2.0 * jnp.pi) ** 1.5
    )
    rows = [
        jnp.ones_like(discrete_abscissa_xaxis),
        discrete_abscissa_xaxis,
        discrete_abscissa_yaxis,
        discrete_abscissa_zaxis,
        square,
        discrete_abscissa_xaxis * discrete_abscissa_xaxis,
        discrete_abscissa_yaxis * discrete_abscissa_yaxis,
        discrete_abscissa_xaxis * discrete_abscissa_yaxis,
        discrete_abscissa_xaxis * discrete_abscissa_zaxis,
        discrete_abscissa_yaxis * discrete_abscissa_zaxis,
        discrete_abscissa_xaxis * square,
        discrete_abscissa_yaxis * square,
        discrete_abscissa_zaxis * square,
    ]
    return jnp.stack(rows) * quadrature


def conserved(moments):
    return jnp.stack([moments[0], moments[1], moments[2], moments[3], 0.5 * moments[4]])


def heat_flux(moments):
    mass = moments[0]
    flow_x = moments[1] / mass
    flow_y = moments[2] / mass
    flow_z = moments[3] / mass
    p_xx = moments[5]
    p_yy = moments[6]
    p_zz = moments[4] - moments[5] - moments[6]
    p_xy = moments[7]
    p_xz = moments[8]
    p_yz = moments[9]
    flow_sq = flow_x * flow_x + flow_y * flow_y + flow_z * flow_z
    heat_x = 0.5 * (
        moments[10]
        - 2.0 * (flow_x * p_xx + flow_y * p_xy + flow_z * p_xz)
        - flow_x * moments[4]
        + 2.0 * mass * flow_sq * flow_x
    )
    heat_y = 0.5 * (
        moments[11]
        - 2.0 * (flow_x * p_xy + flow_y * p_yy + flow_z * p_yz)
        - flow_y * moments[4]
        + 2.0 * mass * flow_sq * flow_y
    )
    heat_z = 0.5 * (
        moments[12]
        - 2.0 * (flow_x * p_xz + flow_y * p_yz + flow_z * p_zz)
        - flow_z * moments[4]
        + 2.0 * mass * flow_sq * flow_z
    )
    return jnp.stack([heat_x, heat_y, heat_z])


def transport(field, courant_x, courant_y):
    from_left = jnp.roll(field, 1, 2)
    from_right = jnp.roll(field, -1, 2)
    term_y = jnp.where(
        courant_y > 0, courant_y * (field - from_left), courant_y * (from_right - field)
    )
    padded = with_halo(field, (("space", 1),), 1)
    term_x = jnp.where(
        courant_x > 0, courant_x * (field - padded[:, :-2]), courant_x * (padded[:, 2:] - field)
    )
    return field - term_x - term_y


def diffuse(source):
    margin = with_halo(source, (("space", 1),), SWEEPS)
    iterate = margin
    for sweep_index in range(SWEEPS):
        inner = iterate[:, 1:-1]
        beside = iterate[:, :-2] + iterate[:, 2:] + jnp.roll(inner, 1, 2) + jnp.roll(inner, -1, 2)
        margin_edge = sweep_index + 1
        iterate = (
            margin[:, margin_edge : margin.shape[1] - margin_edge] + diffusivity * beside
        ) / (1.0 + 4.0 * diffusivity)
    return iterate


def collision_update_piece(
    convected_fields,
    discrete_abscissa_xaxis,
    discrete_abscissa_yaxis,
    discrete_abscissa_zaxis,
    particle_concentration,
    mean_drift_velocity,
    kinetic_thermal_level,
    energy_flux_components,
    collision_frequency,
    obstacle_indicators,
):
    diff_x = discrete_abscissa_xaxis - mean_drift_velocity[0]
    diff_y = discrete_abscissa_yaxis - mean_drift_velocity[1]
    diff_z = discrete_abscissa_zaxis - mean_drift_velocity[2]
    quadratic_deviation = diff_x * diff_x + diff_y * diff_y + diff_z * diff_z
    prefactor_amplitude = particle_concentration * kinetic_thermal_level ** (-1.5)
    local_gaussian_population = prefactor_amplitude * jnp.exp(
        -0.5 * quadratic_deviation / kinetic_thermal_level
    )
    skewed_correction_multiplier = (1.0 - momentum_thermal_ratio) / (
        5.0 * particle_concentration * kinetic_thermal_level * kinetic_thermal_level
    )
    projected_energy_flux = (
        diff_x * energy_flux_components[0]
        + diff_y * energy_flux_components[1]
        + diff_z * energy_flux_components[2]
    )
    goal_population = local_gaussian_population * (
        1.0
        + skewed_correction_multiplier
        * projected_energy_flux
        * (quadratic_deviation / kinetic_thermal_level - 5.0)
    )
    wall_state = particle_concentration * jnp.exp(
        -0.5
        * (
            discrete_abscissa_xaxis * discrete_abscissa_xaxis
            + discrete_abscissa_yaxis * discrete_abscissa_yaxis
            + discrete_abscissa_zaxis * discrete_abscissa_zaxis
        )
    )
    relaxed = convected_fields + collision_frequency * (goal_population - convected_fields)
    return jnp.where(obstacle_indicators > 0, wall_state, relaxed)


def per_device(distribution, rate_class, boundary_obstacle_indicator):
    vel_count, row_count, col_count = distribution.shape
    index = lax.axis_index("vel") * vel_count + jnp.arange(vel_count, dtype=jnp.int32)
    discrete_abscissa_xaxis, discrete_abscissa_yaxis, discrete_abscissa_zaxis = velocity_table(
        index
    )
    weights = moment_weights(
        discrete_abscissa_xaxis, discrete_abscissa_yaxis, discrete_abscissa_zaxis
    )
    column_x = discrete_abscissa_xaxis[:, None, None]
    column_y = discrete_abscissa_yaxis[:, None, None]
    column_z = discrete_abscissa_zaxis[:, None, None]
    courant_x = marching_step_length * column_x
    courant_y = marching_step_length * column_y
    reference_collision_freq = 0.5 * jnp.exp2(rate_class.astype(jnp.float32))
    field = distribution
    latest_conserved_fields = jnp.zeros((5, row_count, col_count), jnp.float32)
    for step_index in range(ITERS):
        convected_fields = transport(field, courant_x, courant_y)
        partial_value = jnp.dot(
            weights,
            convected_fields.reshape(vel_count, row_count * col_count),
            precision=lax.Precision.HIGHEST,
            preferred_element_type=jnp.float32,
        )
        moments = lax.psum(partial_value, "vel")
        source = conserved(moments)
        energy_flux_components = heat_flux(moments)
        source = source.reshape(5, row_count, col_count)
        energy_flux_components = energy_flux_components.reshape(3, row_count, col_count)
        latest_conserved_fields = diffuse(source)
        particle_concentration = latest_conserved_fields[0]
        mean_drift_velocity = latest_conserved_fields[1:4] / particle_concentration
        kinetic_thermal_level = (
            2.0 * latest_conserved_fields[4] / particle_concentration
            - (
                mean_drift_velocity[0] * mean_drift_velocity[0]
                + mean_drift_velocity[1] * mean_drift_velocity[1]
                + mean_drift_velocity[2] * mean_drift_velocity[2]
            )
        ) / 3.0
        collision_frequency = 1.0 - jnp.exp(
            -marching_step_length
            * reference_collision_freq
            * particle_concentration
            * kinetic_thermal_level ** (1.0 - shear_power_law_index)
        )
        field = collision_update_piece(
            convected_fields,
            column_x,
            column_y,
            column_z,
            particle_concentration,
            mean_drift_velocity,
            kinetic_thermal_level,
            energy_flux_components,
            collision_frequency,
            boundary_obstacle_indicator,
        )
    return (field, latest_conserved_fields)


def solution(mesh):
    placed = (P("vel", "space", None), P("space", None), P("space", None))
    return jax.shard_map(
        per_device,
        mesh=mesh,
        in_specs=placed,
        out_specs=(P("vel", "space", None), P(None, "space", None)),
        check_vma=False,
    )
```

profile of v0, /device:TPU:0, one launch (start us, length us, event | category | flops | bytes accessed | tf_op | source)
XLA Modules:
  0.0 239.6 jit_solution(17886712523408883976)
XLA Ops:
  0.6 4.2 %fusion.177 = (f32[1024,1,128]{2,1,0:T(1,128)S(1)}, f32[1024,1,128]{2,1,0:T(1,128)S(1)}) fusion(f32[1024,8,128]{2,1,0:T(8,128)} %param.3), kind=kLoop, calls=%fused_computation.291 | loop fusion | bytes 2097152 | tf_op jit(solution)/shard_map/slice | solution.py:23
  4.8 0.6 collective-permute-start.1
  5.4 0.1 collective-permute-start
  5.5 0.1 multiply_add_fusion
  5.6 0.1 fusion.164
  5.7 0.1 fusion.166
  5.8 0.1 fusion.170
  6.1 5.4 %copy.27 = f32[1024,8,128]{0,2,1:T(8,128)} copy(f32[1024,8,128]{2,1,0:T(8,128)} %param.3) | data formatting | bytes 8388608 | tf_op args[0]
  11.4 1.1 fusion.176
  12.5 0.1 stack.16
  12.6 8.7 %fusion.175 = (f32[1024,8,127]{0,2,1:T(8,128)}, f32[1024,8,127]{0,2,1:T(8,128)}) fusion(f32[1024,8,128]{0,2,1:T(8,128)} %copy.27), kind=kLoop, calls=%fused_computation.289 | loop fusion | bytes 16646144 | tf_op jit(solution)/shard_map/jit(_roll_static)/slice | solution.py:118
  21.4 0.2 copy.25
  21.6 0.2 copy.20
  21.8 8.6 %fusion.47 = f32[1024,8,128]{0,2,1:T(8,128)S(1)} fusion(f32[1024,8,128]{0,2,1:T(8,128)} %copy.27, f32[1024,1,128]{0,2,1:T(8,128)S(1)} %copy.25, f32[1024,1,128]{0,2,1:T(8,128)S(1)} %copy.20, f32[1024,8,127]{0,2,1:T(8,128)} %get-tuple-element.17, f32[1024,8,1]{0,2,1:T(1,128)S(1)} %get-tuple-element.19, f32[1024,8,1]{0,2,1:T(1,128)S(1)} %get-tuple-element.18, ...), kind=kLoop, calls=%fused_computation.62 | loop fusion | flops 16777216 | bytes 17836032 | tf_op jit(solution)/shard_map/sub | solution.py:126
  30.4 2.0 copy-done.2
  32.4 3.6 %fusion.58 = f32[13,1024]{1,0:T(8,128)S(1)} fusion(f32[1024,1024]{0,1:T(8,128)S(1)} %bitcast.95, f32[13,1024]{1,0:T(8,128)S(1)} %stack.16), kind=kOutput, calls=%fused_computation.78 | convolution fusion | flops 163591168 | bytes 4300800 | tf_op jit(solution)/shard_map/dot_general | solution.py:207
  36.0 78.6 %psum.14 = f32[13,1024]{1,0:T(8,128)S(1)} all-reduce(f32[13,1024]{1,0:T(8,128)S(1)} %fusion.58), channel_id=1, replica_groups=mesh['vel'=16,'space'=2] {'vel'}, use_global_device_ids=true, to_apply=%region_0.1 | all-reduce | flops 13312 | bytes 106496 | tf_op jit(solution)/shard_map/psum | solution.py:213
  114.8 0.5 collective-permute-start.3
  115.3 0.6 collective-permute-done.2
  115.9 0.2 collective-permute-done.3
  116.1 0.1 fusion.193
  116.3 0.1 fusion.83
  116.5 0.1 fusion.79
  116.6 0.1 fusion.188
  116.8 0.1 fusion.75
  117.0 0.1 fusion.89
  117.2 7.4 %fusion.11 = f32[1024,8,128]{0,2,1:T(8,128)S(1)} fusion(f32[1024,8,128]{0,2,1:T(8,128)} %copy-done.2, f32[8,128]{1,0:T(8,128)S(1)} %bitcast.117, f32[8,128]{1,0:T(8,128)S(1)} %bitcast.115, f32[8,128]{1,0:T(8,128)S(1)} %bitcast.114, f32[8,128]{1,0:T(8,128)S(1)} %fusion.113, f32[8,128]{1,0:T(8,128)S(1)} %bitcast.111, f32[8,128]{1,0:T(8,128)S(1)} %get-tuple-element.71, ...), kind=kLoop, calls=%fused_computation.23 | loop fusion | flops 28311552 | bytes 8451072 | tf_op jit(solution)/shard_map/jit(_where)/select_n | solution.py:185
  124.7 1.9 copy-done
  126.7 0.2 copy.34
  126.9 0.2 copy.36
  127.1 0.4 collective-permute-start.5
  127.5 0.2 collective-permute-start.4
  127.7 8.7 %fusion.172 = (f32[1024,8,127]{0,2,1:T(8,128)}, f32[1024,8,127]{0,2,1:T(8,128)}) fusion(f32[1024,8,128]{0,2,1:T(8,128)} %copy-done), kind=kLoop, calls=%fused_computation.286 | loop fusion | bytes 16646144 | tf_op jit(solution)/shard_map/jit(_roll_static)/slice | solution.py:118
  136.5 0.2 copy.37
  136.7 0.2 copy.35
  136.9 8.6 %fusion.40 = f32[1024,8,128]{0,2,1:T(8,128)S(1)} fusion(f32[1024,8,128]{0,2,1:T(8,128)} %copy-done, f32[1024,1,128]{0,2,1:T(8,128)S(1)} %copy.37, f32[1024,1,128]{0,2,1:T(8,128)S(1)} %copy.35, f32[1024,8,127]{0,2,1:T(8,128)} %get-tuple-element.11, f32[1024,8,1]{0,2,1:T(1,128)S(1)} %get-tuple-element.13, f32[1024,8,1]{0,2,1:T(1,128)S(1)} %get-tuple-element.12, ...), kind=kLoop, calls=%fused_computation.53 | loop fusion | flops 16777216 | bytes 17836032 | tf_op jit(solution)/shard_map/sub | solution.py:126
  145.5 2.0 copy-done.1
  147.5 3.6 %fusion.56 = f32[13,1024]{1,0:T(8,128)S(1)} fusion(f32[1024,1024]{0,1:T(8,128)S(1)} %bitcast.94, f32[13,1024]{1,0:T(8,128)S(1)} %stack.16), kind=kOutput, calls=%fused_computation.76 | convolution fusion | flops 163591168 | bytes 4300800 | tf_op jit(solution)/shard_map/dot_general | solution.py:207
  151.1 71.8 %psum.15 = f32[13,1024]{1,0:T(8,128)S(1)} all-reduce(f32[13,1024]{1,0:T(8,128)S(1)} %fusion.56), channel_id=1, replica_groups=mesh['vel'=16,'space'=2] {'vel'}, use_global_device_ids=true, to_apply=%region_1.2 | all-reduce | flops 13312 | bytes 106496 | tf_op jit(solution)/shard_map/psum | solution.py:213
  223.0 0.5 collective-permute-start.7
  223.6 0.6 collective-permute-done.6
  224.2 0.2 collective-permute-done.7
  224.5 0.1 fusion.71
  224.8 0.1 fusion.67
  225.0 0.1 fusion.63
  225.3 0.1 fusion.87
  225.5 8.8 %fusion.29 = f32[1024,8,128]{0,2,1:T(8,128)} fusion(f32[1024,8,128]{0,2,1:T(8,128)} %copy-done.1, f32[8,128]{1,0:T(8,128)S(1)} %bitcast.116, f32[8,128]{1,0:T(8,128)S(1)} %bitcast.113, f32[8,128]{1,0:T(8,128)S(1)} %bitcast.112, f32[8,128]{1,0:T(8,128)S(1)} %fusion.115, f32[8,128]{1,0:T(8,128)S(1)} %bitcast.110, f32[8,128]{1,0:T(8,128)S(1)} %get-tuple-element.68, ...), kind=kLoop, calls=%fused_computation.41 | loop fusion | flops 28311552 | bytes 8451072 | tf_op jit(solution)/shard_map/jit(_where)/select_n | solution.py:185
  234.3 5.4 %copy.38 = f32[1024,8,128]{2,1,0:T(8,128)} copy(f32[1024,8,128]{0,2,1:T(8,128)} %fusion.29) | data formatting | bytes 8388608
  (61 shorter events, 2.0 us)
Async XLA Ops:
  4.8 16.6 %collective-permute-start.1 = (f32[1024,1,128]{2,0,1:T(8,128)S(1)}, f32[1024,1,128]{2,0,1:T(8,128)S(1)}, u32[]{:S(2)}, u32[]{:S(2)}) collective-permute-start(f32[1024,1,128]{2,0,1:T(8,128)S(1)} %bitcast.97), channel_id=1, source_target_pairs={{1,0},{0,1},{3,2},{2,3},{5,4},{4,5},{7,6},{6,7},{9,8},{8,9},{11,10... | collective-permute-start | bytes 1572872 | tf_op jit(solution)/shard_map/ppermute | solution.py:26
  5.4 16.2 %collective-permute-start = (f32[1024,1,128]{2,0,1:T(8,128)S(1)}, f32[1024,1,128]{2,0,1:T(8,128)S(1)}, u32[]{:S(2)}, u32[]{:S(2)}) collective-permute-start(f32[1024,1,128]{2,0,1:T(8,128)S(1)} %bitcast.96), channel_id=1, source_target_pairs={{0,1},{1,0},{2,3},{3,2},{4,5},{5,4},{6,7},{7,6},{8,9},{9,8},{10,11... | collective-permute-start | bytes 1572872 | tf_op jit(solution)/shard_map/ppermute | solution.py:25
  6.1 5.4 %copy-start.5 = (s32[8,128]{1,0:T(8,128)S(1)}, s32[8,128]{1,0:T(8,128)}, u32[]{:S(2)}) copy-start(s32[8,128]{1,0:T(8,128)} %param.5) | copy-start | bytes 12292
  30.4 2.0 copy-start.2
  30.4 86.7 %copy-start.4 = (s32[8,128]{1,0:T(8,128)S(1)}, s32[8,128]{1,0:T(8,128)}, u32[]{:S(2)}) copy-start(s32[8,128]{1,0:T(8,128)} %param.4) | copy-start | bytes 12292
  114.7 1.2 collective-permute-start.2
  114.8 1.3 collective-permute-start.3
  124.6 2.0 copy-start
  127.1 9.3 %collective-permute-start.5 = (f32[1024,1,128]{2,0,1:T(8,128)S(1)}, f32[1024,1,128]{2,0,1:T(8,128)S(1)}, u32[]{:S(2)}, u32[]{:S(2)}) collective-permute-start(f32[1024,1,128]{2,0,1:T(8,128)S(1)} %copy.36), channel_id=1, source_target_pairs={{1,0},{0,1},{3,2},{2,3},{5,4},{4,5},{7,6},{6,7},{9,8},{8,9},{11,10... | collective-permute-start | bytes 1572872 | tf_op jit(solution)/shard_map/ppermute | solution.py:26
  127.5 9.1 %collective-permute-start.4 = (f32[1024,1,128]{2,0,1:T(8,128)S(1)}, f32[1024,1,128]{2,0,1:T(8,128)S(1)}, u32[]{:S(2)}, u32[]{:S(2)}) collective-permute-start(f32[1024,1,128]{2,0,1:T(8,128)S(1)} %copy.34), channel_id=1, source_target_pairs={{0,1},{1,0},{2,3},{3,2},{4,5},{5,4},{6,7},{7,6},{8,9},{9,8},{10,11... | collective-permute-start | bytes 1572872 | tf_op jit(solution)/shard_map/ppermute | solution.py:25
  145.5 2.0 copy-start.1
  222.9 1.2 collective-permute-start.6
  223.0 1.3 collective-permute-start.7
  225.4 8.9 %copy-start.3 = (f32[5,8,128]{2,1,0:T(8,128)}, f32[5,8,128]{2,1,0:T(8,128)S(1)}, u32[]{:S(2)}) copy-start(f32[5,8,128]{2,1,0:T(8,128)S(1)} %fusion.87) | copy-start | bytes 61444
where the time goes:
time: 240 us
  blocking collectives  150 us (62%)
  local copies, waits for them, and re-layouts  42.1 us (18%)
  other arithmetic  35.1 us (15%)
  matrix products  7.12 us (3%)
    psum x2, blocking collectives, per_device(): moments = lax.psum(partial_value, 'vel')  150 us
    slice x4, local copies, waits for them, and re-layouts, transport(): from_right = jnp.roll(field, -1, 2)  18.6 us
    sub x2, other arithmetic, transport(): return field - term_x - term_y  17.2 us
    unnamed x18, local copies, waits for them, and re-layouts  16.7 us
    select_n x2, other arithmetic, collision_update_piece(): return jnp.where(obstacle_indicators > 0, wall_state, relaxed)  16.2 us
    dot_general x2, matrix products, per_device(): jnp.dot(weights, convected_fields.reshape(vel_count, row_count * col_coun...  7.12 us
  transfers between devices with their start and end apart: 8, of which 4 were waited for; matrix products, arithmetic and copies ran while one was open for 10% of the time, Pallas kernels for 0%

commit v1 on v0

--- a/solution.py
+++ b/solution.py
@@ -210,7 +210,7 @@
             precision=lax.Precision.HIGHEST,
             preferred_element_type=jnp.float32,
         )
-        moments = lax.psum(partial_value, "vel")
+        moments = jnp.sum(lax.all_gather(partial_value, "vel"), axis=0)
         source = conserved(moments)
         energy_flux_components = heat_flux(moments)
         source = source.reshape(5, row_count, col_count)

time: 240 us -> 181 us (0.75)
  blocking collectives: 150 us -> 90.8 us
    psum x2 -> x0, blocking collectives: 150 us -> none  [per_device(): moments = lax.psum(partial_value, 'vel')]
    all_gather x0 -> x2, blocking collectives: none -> 90.8 us  [per_device(): moments = jnp.sum(lax.all_gather(partial_value, 'vel'), axis=0)]
  transfers between devices with their start and end apart: 8 -> 8, of which waited for: 4 -> 4; matrix products, arithmetic and copies ran while one was open for 10% -> 14% of each run, Pallas kernels for 0% -> 0%
where the time goes in v1:
time: 181 us; the launch traced here: 180 us
  blocking collectives  90.8 us (50%)
  local copies, waits for them, and re-layouts  42.1 us (23%)
  other arithmetic  35.3 us (20%)
  matrix products  7.12 us (4%)
  starting transfers between devices  2.35 us (1%)
    all_gather x2, blocking collectives, per_device(): moments = jnp.sum(lax.all_gather(partial_value, 'vel'), axis=0)  90.8 us
    slice x4, local copies, waits for them, and re-layouts, transport(): from_right = jnp.roll(field, -1, 2)  18.6 us
    sub x2, other arithmetic, transport(): return field - term_x - term_y  17.2 us
    unnamed x18, local copies, waits for them, and re-layouts  16.7 us
    select_n x2, other arithmetic, collision_update_piece(): return jnp.where(obstacle_indicators > 0, wall_state, relaxed)  16.2 us
    dot_general x2, matrix products, per_device(): jnp.dot(weights, convected_fields.reshape(vel_count, row_count * col_coun...  7.12 us
    slice x3, local copies, waits for them, and re-layouts, with_halo(): last = lax.slice_in_dim(value, length - width, length, axis=dim)  4.45 us
  transfers between devices with their start and end apart: 8, of which 4 were waited for; matrix products, arithmetic and copies ran while one was open for 14% of the time, Pallas kernels for 0%

profile of v1, /device:TPU:0, one launch (start us, length us, event | category | flops | bytes accessed | tf_op | source)
XLA Modules:
  0.0 180.3 jit_solution(12490442037761716975)
XLA Ops:
  0.6 4.2 %fusion.175 = (f32[1024,1,128]{2,1,0:T(1,128)S(1)}, f32[1024,1,128]{2,1,0:T(1,128)S(1)}) fusion(f32[1024,8,128]{2,1,0:T(8,128)} %param.3), kind=kLoop, calls=%fused_computation.291 | loop fusion | bytes 2097152 | tf_op jit(solution)/shard_map/slice | solution.py:23
  4.8 0.6 collective-permute-start.1
  5.4 0.1 collective-permute-start
  5.5 0.1 multiply_add_fusion
  5.6 0.1 fusion.162
  5.7 0.1 fusion.164
  5.8 0.1 fusion.168
  6.1 5.4 %copy.27 = f32[1024,8,128]{0,2,1:T(8,128)} copy(f32[1024,8,128]{2,1,0:T(8,128)} %param.3) | data formatting | bytes 8388608 | tf_op args[0]
  11.4 1.1 fusion.174
  12.5 0.1 stack.16
  12.6 8.7 %fusion.173 = (f32[1024,8,127]{0,2,1:T(8,128)}, f32[1024,8,127]{0,2,1:T(8,128)}) fusion(f32[1024,8,128]{0,2,1:T(8,128)} %copy.27), kind=kLoop, calls=%fused_computation.289 | loop fusion | bytes 16646144 | tf_op jit(solution)/shard_map/jit(_roll_static)/slice | solution.py:118
  21.4 0.2 copy.25
  21.6 0.2 copy.20
  21.8 8.6 %fusion.47 = f32[1024,8,128]{0,2,1:T(8,128)S(1)} fusion(f32[1024,8,128]{0,2,1:T(8,128)} %copy.27, f32[1024,1,128]{0,2,1:T(8,128)S(1)} %copy.25, f32[1024,1,128]{0,2,1:T(8,128)S(1)} %copy.20, f32[1024,8,127]{0,2,1:T(8,128)} %get-tuple-element.17, f32[1024,8,1]{0,2,1:T(1,128)S(1)} %get-tuple-element.19, f32[1024,8,1]{0,2,1:T(1,128)S(1)} %get-tuple-element.18, ...), kind=kLoop, calls=%fused_computation.62 | loop fusion | flops 16777216 | bytes 17836032 | tf_op jit(solution)/shard_map/sub | solution.py:126
  30.4 2.0 %copy-done.2 = f32[1024,8,128]{0,2,1:T(8,128)} copy-done((f32[1024,8,128]{0,2,1:T(8,128)}, f32[1024,8,128]{0,2,1:T(8,128)S(1)}, u32[]{:S(2)}) %copy-start.2) | copy-done | bytes 4194328
  32.4 3.6 %convolution_bitcast_fusion.1 = f32[1,13,1024]{2,1,0:T(8,128)S(1)} fusion(f32[1024,1024]{0,1:T(8,128)S(1)} %bitcast.99, f32[13,1024]{1,0:T(8,128)S(1)} %stack.16), kind=kOutput, calls=%fused_computation.77 | convolution fusion | flops 163591168 | bytes 4300800 | tf_op jit(solution)/shard_map/dot_general | solution.py:207
  36.0 49.3 %all-gather.2 = f32[16,13,1024]{2,1,0:T(8,128)S(1)} all-gather(f32[1,13,1024]{2,1,0:T(8,128)S(1)} %convolution_bitcast_fusion.1), channel_id=2, replica_groups=mesh['vel'=16,'space'=2] {'vel'}, dimensions={0}, use_global_device_ids=true | all-gather | bytes 905216 | tf_op jit(solution)/shard_map/all_gather | solution.py:213
  85.5 0.5 collective-permute-start.3
  86.1 0.6 collective-permute-done.2
  86.7 0.2 collective-permute-done.3
  86.8 0.1 fusion.191
  87.0 0.1 fusion.81
  87.1 0.1 fusion.188
  87.3 0.1 fusion.77
  87.5 0.1 fusion.73
  87.8 0.1 fusion.87
  88.0 7.4 %fusion.11 = f32[1024,8,128]{0,2,1:T(8,128)S(1)} fusion(f32[1024,8,128]{0,2,1:T(8,128)} %copy-done.2, f32[8,128]{1,0:T(8,128)S(1)} %bitcast.121, f32[8,128]{1,0:T(8,128)S(1)} %bitcast.119, f32[8,128]{1,0:T(8,128)S(1)} %bitcast.118, f32[8,128]{1,0:T(8,128)S(1)} %fusion.111, f32[8,128]{1,0:T(8,128)S(1)} %bitcast.115, f32[8,128]{1,0:T(8,128)S(1)} %get-tuple-element.71, ...), kind=kLoop, calls=%fused_computation.23 | loop fusion | flops 28311552 | bytes 8451072 | tf_op jit(solution)/shard_map/jit(_where)/select_n | solution.py:185
  95.5 1.9 %copy-done = f32[1024,8,128]{0,2,1:T(8,128)} copy-done((f32[1024,8,128]{0,2,1:T(8,128)}, f32[1024,8,128]{0,2,1:T(8,128)S(1)}, u32[]{:S(2)}) %copy-start) | copy-done | bytes 4194328
  97.5 0.2 copy.34
  97.7 0.2 copy.36
  97.9 0.4 collective-permute-start.5
  98.3 0.2 collective-permute-start.4
  98.5 8.7 %fusion.170 = (f32[1024,8,127]{0,2,1:T(8,128)}, f32[1024,8,127]{0,2,1:T(8,128)}) fusion(f32[1024,8,128]{0,2,1:T(8,128)} %copy-done), kind=kLoop, calls=%fused_computation.286 | loop fusion | bytes 16646144 | tf_op jit(solution)/shard_map/jit(_roll_static)/slice | solution.py:118
  107.2 0.2 copy.37
  107.4 0.2 copy.35
  107.6 8.6 %fusion.40 = f32[1024,8,128]{0,2,1:T(8,128)S(1)} fusion(f32[1024,8,128]{0,2,1:T(8,128)} %copy-done, f32[1024,1,128]{0,2,1:T(8,128)S(1)} %copy.37, f32[1024,1,128]{0,2,1:T(8,128)S(1)} %copy.35, f32[1024,8,127]{0,2,1:T(8,128)} %get-tuple-element.11, f32[1024,8,1]{0,2,1:T(1,128)S(1)} %get-tuple-element.13, f32[1024,8,1]{0,2,1:T(1,128)S(1)} %get-tuple-element.12, ...), kind=kLoop, calls=%fused_computation.53 | loop fusion | flops 16777216 | bytes 17836032 | tf_op jit(solution)/shard_map/sub | solution.py:126
  116.2 2.0 %copy-done.1 = f32[1024,8,128]{0,2,1:T(8,128)} copy-done((f32[1024,8,128]{0,2,1:T(8,128)}, f32[1024,8,128]{0,2,1:T(8,128)S(1)}, u32[]{:S(2)}) %copy-start.1) | copy-done | bytes 4194328
  118.2 3.6 %convolution_bitcast_fusion = f32[1,13,1024]{2,1,0:T(8,128)S(1)} fusion(f32[1024,1024]{0,1:T(8,128)S(1)} %bitcast.98, f32[13,1024]{1,0:T(8,128)S(1)} %stack.16), kind=kOutput, calls=%fused_computation.76 | convolution fusion | flops 163591168 | bytes 4300800 | tf_op jit(solution)/shard_map/dot_general | solution.py:207
  121.8 41.6 %all-gather.3 = f32[16,13,1024]{2,1,0:T(8,128)S(1)} all-gather(f32[1,13,1024]{2,1,0:T(8,128)S(1)} %convolution_bitcast_fusion), channel_id=3, replica_groups=mesh['vel'=16,'space'=2] {'vel'}, dimensions={0}, use_global_device_ids=true | all-gather | bytes 905216 | tf_op jit(solution)/shard_map/all_gather | solution.py:213
  163.6 0.5 collective-permute-start.7
  164.2 0.6 collective-permute-done.6
  164.8 0.2 collective-permute-done.7
  165.1 0.1 fusion.69
  165.4 0.1 fusion.65
  165.6 0.1 fusion.61
  165.9 0.1 fusion.85
  166.1 8.8 %fusion.29 = f32[1024,8,128]{0,2,1:T(8,128)} fusion(f32[1024,8,128]{0,2,1:T(8,128)} %copy-done.1, f32[8,128]{1,0:T(8,128)S(1)} %bitcast.120, f32[8,128]{1,0:T(8,128)S(1)} %bitcast.117, f32[8,128]{1,0:T(8,128)S(1)} %bitcast.116, f32[8,128]{1,0:T(8,128)S(1)} %fusion.113, f32[8,128]{1,0:T(8,128)S(1)} %bitcast.114, f32[8,128]{1,0:T(8,128)S(1)} %get-tuple-element.68, ...), kind=kLoop, calls=%fused_computation.41 | loop fusion | flops 28311552 | bytes 8451072 | tf_op jit(solution)/shard_map/jit(_where)/select_n | solution.py:185
  174.9 5.4 %copy.38 = f32[1024,8,128]{2,1,0:T(8,128)} copy(f32[1024,8,128]{0,2,1:T(8,128)} %fusion.29) | data formatting | bytes 8388608
  (63 shorter events, 2.1 us)
Async XLA Ops:
  4.8 16.6 %collective-permute-start.1 = (f32[1024,1,128]{2,0,1:T(8,128)S(1)}, f32[1024,1,128]{2,0,1:T(8,128)S(1)}, u32[]{:S(2)}, u32[]{:S(2)}) collective-permute-start(f32[1024,1,128]{2,0,1:T(8,128)S(1)} %bitcast.101), channel_id=1, source_target_pairs={{1,0},{0,1},{3,2},{2,3},{5,4},{4,5},{7,6},{6,7},{9,8},{8,9},{11,10... | collective-permute-start | bytes 1572872 | tf_op jit(solution)/shard_map/ppermute | solution.py:26
  5.4 16.2 %collective-permute-start = (f32[1024,1,128]{2,0,1:T(8,128)S(1)}, f32[1024,1,128]{2,0,1:T(8,128)S(1)}, u32[]{:S(2)}, u32[]{:S(2)}) collective-permute-start(f32[1024,1,128]{2,0,1:T(8,128)S(1)} %bitcast.100), channel_id=1, source_target_pairs={{0,1},{1,0},{2,3},{3,2},{4,5},{5,4},{6,7},{7,6},{8,9},{9,8},{10,11... | collective-permute-start | bytes 1572872 | tf_op jit(solution)/shard_map/ppermute | solution.py:25
  6.1 5.4 %copy-start.5 = (s32[8,128]{1,0:T(8,128)S(1)}, s32[8,128]{1,0:T(8,128)}, u32[]{:S(2)}) copy-start(s32[8,128]{1,0:T(8,128)} %param.5) | copy-start | bytes 12292
  30.4 2.0 %copy-start.2 = (f32[1024,8,128]{0,2,1:T(8,128)}, f32[1024,8,128]{0,2,1:T(8,128)S(1)}, u32[]{:S(2)}) copy-start(f32[1024,8,128]{0,2,1:T(8,128)S(1)} %fusion.47) | copy-start | bytes 12582916
  32.4 55.5 %copy-start.4 = (s32[8,128]{1,0:T(8,128)S(1)}, s32[8,128]{1,0:T(8,128)}, u32[]{:S(2)}) copy-start(s32[8,128]{1,0:T(8,128)} %param.4) | copy-start | bytes 12292
  85.4 1.2 collective-permute-start.2
  85.5 1.3 collective-permute-start.3
  95.4 2.0 %copy-start = (f32[1024,8,128]{0,2,1:T(8,128)}, f32[1024,8,128]{0,2,1:T(8,128)S(1)}, u32[]{:S(2)}) copy-start(f32[1024,8,128]{0,2,1:T(8,128)S(1)} %fusion.11) | copy-start | bytes 12582916
  97.9 9.3 %collective-permute-start.5 = (f32[1024,1,128]{2,0,1:T(8,128)S(1)}, f32[1024,1,128]{2,0,1:T(8,128)S(1)}, u32[]{:S(2)}, u32[]{:S(2)}) collective-permute-start(f32[1024,1,128]{2,0,1:T(8,128)S(1)} %copy.36), channel_id=1, source_target_pairs={{1,0},{0,1},{3,2},{2,3},{5,4},{4,5},{7,6},{6,7},{9,8},{8,9},{11,10... | collective-permute-start | bytes 1572872 | tf_op jit(solution)/shard_map/ppermute | solution.py:26
  98.3 9.1 %collective-permute-start.4 = (f32[1024,1,128]{2,0,1:T(8,128)S(1)}, f32[1024,1,128]{2,0,1:T(8,128)S(1)}, u32[]{:S(2)}, u32[]{:S(2)}) collective-permute-start(f32[1024,1,128]{2,0,1:T(8,128)S(1)} %copy.34), channel_id=1, source_target_pairs={{0,1},{1,0},{2,3},{3,2},{4,5},{5,4},{6,7},{7,6},{8,9},{9,8},{10,11... | collective-permute-start | bytes 1572872 | tf_op jit(solution)/shard_map/ppermute | solution.py:25
  116.2 2.0 %copy-start.1 = (f32[1024,8,128]{0,2,1:T(8,128)}, f32[1024,8,128]{0,2,1:T(8,128)S(1)}, u32[]{:S(2)}) copy-start(f32[1024,8,128]{0,2,1:T(8,128)S(1)} %fusion.40) | copy-start | bytes 12582916
  163.5 1.2 collective-permute-start.6
  163.6 1.3 collective-permute-start.7
  166.0 8.9 %copy-start.3 = (f32[5,8,128]{2,1,0:T(8,128)}, f32[5,8,128]{2,1,0:T(8,128)S(1)}, u32[]{:S(2)}) copy-start(f32[5,8,128]{2,1,0:T(8,128)S(1)} %fusion.85) | copy-start | bytes 61444
